TPU v7x, 512 devices: a whole 4x4x16 slice. The times are simulated.
512 devices in a mesh: tok: 32 (over z_hi, y, core), feat: 16 (over x, z_lo).
Axes of the slice: x: 4, y: 4, z: 16 (z_hi: 4, z_lo: 4; z = z_hi * 4 + z_lo), core: 2. Of those that a mesh axis runs over, the one named last changes fastest.
Arguments:
- calib: float32 [5120, 28672], P('tok', 'feat'), may hold values from -6 to 6
- weight: float32 [28672, 512], P('feat', 'tok'), may hold values from -0.03125 to 0.03125
Outputs:
- gram_product: float32 [512, 28672], P('tok', 'feat')
All inputs are finite; a program needn't handle non-finite values.
Results may differ from a plain program's by a relative error of at most 0.000098.
Values sent between devices are 32-bit elements; how exact they have to be, the bound alone decides.
A program may use at most 64 MiB of HBM per device.

v0:
```python
import math
import jax
import jax.numpy as jnp
from jax import lax
from jax.sharding import PartitionSpec as P


def shards(calib, weight):
    tokens_all = calib.shape[0] * lax.axis_size("tok")
    partial_rows = jnp.dot(
        calib,
        lax.all_gather(weight, "tok", axis=1, tiled=True),
        precision=lax.Precision.HIGHEST,
        preferred_element_type=jnp.float32,
    )
    mixed = lax.psum(partial_rows, "feat")
    factor = 1.0 / math.sqrt(tokens_all)
    term = lax.dot_general(
        mixed,
        calib,
        (((0,), (0,)), ((), ())),
        precision=lax.Precision.HIGHEST,
        preferred_element_type=jnp.float32,
    )
    return lax.psum_scatter(term * factor, "tok", scatter_dimension=0, tiled=True)


def solution(mesh):
    return jax.shard_map(
        shards,
        mesh=mesh,
        in_specs=(P("tok", "feat"), P("feat", "tok")),
        out_specs=P("tok", "feat"),
        check_vma=False,
    )
```

profile of v0, /device:TPU:4, one launch (start us, length us, event | category | flops | bytes accessed | tf_op | source)
XLA Modules:
  0.0 423.2 jit_solution(11789714599147911102)
XLA Ops:
  6.5 0.0 copy-start
  6.5 0.0 all-gather.2.cloned.1.call-start
  6.5 0.7 all-gather.2.cloned.1.call-update
  7.3 0.0 all-reduce.2.cloned.1.call-start
  7.3 98.3 %all-gather.2.cloned.1.call-done = f32[1792,512]{0,1:T(8,128)} async-done(((f32[1792,16]{0,1:T(8,128)}), f32[1792,512]{0,1:T(8,128)}) %all-gather.2.cloned.1.call-update) | async-done | bytes 3670032 | tf_op jit(solution)/shard_map/all_gather | solution.py:12
  105.6 0.0 copy-done
  105.6 6.6 %fusion = f32[160,512]{1,0:T(8,128)} fusion(f32[160,1792]{1,0:T(8,128)S(1)} %copy-done, f32[1792,512]{0,1:T(8,128)} %all-gather.2.cloned.1.call-done), kind=kOutput, calls=%fused_computation.1 | convolution fusion | flops 1761607680 | bytes 5144576 | tf_op jit(solution)/shard_map/dot_general | solution.py:10
  112.2 0.0 all-reduce.2.cloned.1.call-update
  112.2 0.0 reduce-scatter.2.cloned.1.call-start
  112.3 156.4 %all-reduce.2.cloned.1.call-done = f32[160,512]{1,0:T(8,128)} async-done(((f32[160,512]{1,0:T(8,128)}), f32[160,512]{1,0:T(8,128)}) %all-reduce.2.cloned.1.call-update) | async-done | bytes 327696 | tf_op jit(solution)/shard_map/psum | solution.py:16
  268.7 5.9 %convolution_multiply_fusion = f32[512,1792]{1,0:T(8,128)} fusion(f32[160,512]{1,0:T(8,128)} %all-reduce.2.cloned.1.call-done, f32[160,1792]{1,0:T(8,128)S(1)} %copy-done), kind=kOutput, calls=%fused_computation | convolution fusion | flops 1762525184 | bytes 5144576 | tf_op jit(solution)/shard_map/dot_general | solution.py:18
  274.6 0.0 reduce-scatter.2.cloned.1.call-update
  274.6 142.1 %reduce-scatter.2.cloned.1.call-done = f32[16,1792]{1,0:T(8,128)} async-done(((f32[512,1792]{1,0:T(8,128)}), f32[16,1792]{1,0:T(8,128)}) %reduce-scatter.2.cloned.1.call-update) | async-done | bytes 114704 | tf_op jit(solution)/shard_map/reduce_scatter | solution.py:25
Async XLA Ops:
  6.5 99.1 %copy-start = (f32[160,1792]{1,0:T(8,128)S(1)}, f32[160,1792]{1,0:T(8,128)}, u32[]{:S(2)}) copy-start(f32[160,1792]{1,0:T(8,128)} %param.2) | copy-start | bytes 3440644
  6.5 99.1 %all-gather.2.cloned.1.call-start = ((), (), s32[]{:S(2)}) async-start(), calls=%async_computation.1 | async-start | bytes 3784704 | tf_op jit(solution)/shard_map/all_gather | solution.py:12
  7.3 261.4 %all-reduce.2.cloned.1.call-start = ((), (), s32[]{:S(2)}) async-start(), calls=%async_computation.2 | async-start | bytes 655360 | tf_op jit(solution)/shard_map/psum | solution.py:16
  112.2 304.5 %reduce-scatter.2.cloned.1.call-start = ((), (), s32[]{:S(2)}) async-start(), calls=%async_computation.3 | async-start | bytes 3784704 | tf_op jit(solution)/shard_map/reduce_scatter | solution.py:25
Sparse Core Ops, SparseCore 0:
  10.5 95.1 all-gather.1
  112.3 156.3 all-reduce.1
  274.7 141.9 reduce-scatter.1
where the time goes:
time: 423 us
  waiting for transfers between devices  398 us (94%)
  between operations  13.1 us (3%)
  matrix products  12.4 us (3%)
    psum x1, waiting for transfers between devices, shards(): mixed = lax.psum(partial_rows, 'feat')  156 us
    reduce_scatter x1, waiting for transfers between devices, shards(): lax.psum_scatter(term * factor, 'tok', scatter_dimension=0, tiled=True)  142 us
    all_gather x1, waiting for transfers between devices, shards(): lax.all_gather(weight, 'tok', axis=1, tiled=True)  98.3 us
  transfers between devices with their start and end apart: 3, of which 3 were waited for; matrix products, arithmetic and copies ran while one was open for 0% of the time, Pallas kernels for 0%

commit v1 on v0

--- a/solution.py
+++ b/solution.py
@@ -5,11 +5,16 @@
 from jax.sharding import PartitionSpec as P
 
 
+def exchange_gather(value, axis, d):
+    sent = jnp.stack([value] * lax.axis_size(axis))
+    return jnp.concatenate(lax.all_to_all(sent, axis, 0, 0), axis=d)
+
+
 def shards(calib, weight):
     tokens_all = calib.shape[0] * lax.axis_size("tok")
     partial_rows = jnp.dot(
         calib,
-        lax.all_gather(weight, "tok", axis=1, tiled=True),
+        exchange_gather(weight, "tok", 1),
         precision=lax.Precision.HIGHEST,
         preferred_element_type=jnp.float32,
     )

time: 423 us -> 507 us (1.20)
  blocking collectives: 0 us -> 183 us
  waiting for transfers between devices: 398 us -> 298 us
    all_to_all x0 -> x1, blocking collectives: none -> 183 us  [exchange_gather(): return jnp.concatenate(lax.all_to_all(sent, axis, 0, 0), axis=d)]
    all_gather x1 -> x0, waiting for transfers between devices: 98.3 us -> none  [shards(): lax.all_gather(weight, 'tok', axis=1, tiled=True)]
  transfers between devices with their start and end apart: 3 -> 2, of which waited for: 3 -> 2; matrix products, arithmetic and copies ran while one was open for 0% -> 0% of each run, Pallas kernels for 0% -> 0%
where the time goes in v1:
time: 507 us
  waiting for transfers between devices  298 us (59%)
  blocking collectives  183 us (36%)
  between operations  13.4 us (3%)
  matrix products  10.4 us (2%)
    all_to_all x1, blocking collectives, exchange_gather(): return jnp.concatenate(lax.all_to_all(sent, axis, 0, 0), axis=d)  183 us
    psum x1, waiting for transfers between devices, shards(): mixed = lax.psum(partial_rows, 'feat')  156 us
    reduce_scatter x1, waiting for transfers between devices, shards(): lax.psum_scatter(term * factor, 'tok', scatter_dimension=0, tiled=True)  142 us
  transfers between devices with their start and end apart: 2, of which 2 were waited for; matrix products, arithmetic and copies ran while one was open for 0% of the time, Pallas kernels for 0%

profile of v1, /device:TPU:4, one launch (start us, length us, event | category | flops | bytes accessed | tf_op | source)
XLA Modules:
  0.0 506.9 jit_solution(18007573054753200745)
XLA Ops:
  6.5 0.0 copy-start
  6.5 0.0 all-reduce.2.cloned.1.call-start
  6.5 1.4 stack.2
  7.9 183.4 %all_to_all.5 = f32[32,1792,16]{1,2,0:T(8,128)S(1)} all-to-all(f32[32,1792,16]{1,2,0:T(8,128)S(1)} %stack.2), channel_id=1, replica_groups=mesh['tok'=32,'feat'=16] {'tok'}, dimensions={0} | all-to-all | bytes 7340032 | tf_op jit(solution)/shard_map/all_to_all | solution.py:10
  191.4 0.0 copy-done
  191.4 4.5 fusion
  195.9 0.0 all-reduce.2.cloned.1.call-update
  196.0 0.0 reduce-scatter.2.cloned.1.call-start
  196.0 156.4 %all-reduce.2.cloned.1.call-done = f32[160,512]{1,0:T(8,128)} async-done(((f32[160,512]{1,0:T(8,128)}), f32[160,512]{1,0:T(8,128)}) %all-reduce.2.cloned.1.call-update) | async-done | bytes 327696 | tf_op jit(solution)/shard_map/psum | solution.py:21
  352.4 5.9 %convolution_multiply_fusion = f32[512,1792]{1,0:T(8,128)} fusion(f32[160,512]{1,0:T(8,128)} %all-reduce.2.cloned.1.call-done, f32[160,1792]{1,0:T(8,128)S(1)} %copy-done), kind=kOutput, calls=%fused_computation | convolution fusion | flops 1762525184 | bytes 5144576 | tf_op jit(solution)/shard_map/dot_general | solution.py:23
  358.3 0.0 reduce-scatter.2.cloned.1.call-update
  358.3 141.8 %reduce-scatter.2.cloned.1.call-done = f32[16,1792]{1,0:T(8,128)} async-done(((f32[512,1792]{1,0:T(8,128)}), f32[16,1792]{1,0:T(8,128)}) %reduce-scatter.2.cloned.1.call-update) | async-done | bytes 114704 | tf_op jit(solution)/shard_map/reduce_scatter | solution.py:30
Async XLA Ops:
  6.5 184.9 %copy-start = (f32[160,1792]{1,0:T(8,128)S(1)}, f32[160,1792]{1,0:T(8,128)}, u32[]{:S(2)}) copy-start(f32[160,1792]{1,0:T(8,128)} %param.2) | copy-start | bytes 3440644
  6.5 345.9 %all-reduce.2.cloned.1.call-start = ((), (), s32[]{:S(2)}) async-start(), calls=%async_computation.2 | async-start | bytes 655360 | tf_op jit(solution)/shard_map/psum | solution.py:21
  196.0 304.1 %reduce-scatter.2.cloned.1.call-start = ((), (), s32[]{:S(2)}) async-start(), calls=%async_computation.3 | async-start | bytes 3784704 | tf_op jit(solution)/shard_map/reduce_scatter | solution.py:30
Sparse Core Ops, SparseCore 0:
  196.1 156.2 all-reduce.1
  358.4 141.6 reduce-scatter.1

commit v2 on v0

--- a/solution.py
+++ b/solution.py
@@ -13,7 +13,7 @@
         precision=lax.Precision.HIGHEST,
         preferred_element_type=jnp.float32,
     )
-    mixed = lax.psum(partial_rows, "feat")
+    mixed = jnp.sum(lax.all_gather(partial_rows, axis_name="feat"), 0)
     factor = 1.0 / math.sqrt(tokens_all)
     term = lax.dot_general(
         mixed,

time: 423 us -> 385 us (0.910)
  the two profiles are of different devices: /device:TPU:4 before, /device:TPU:6 now
where the time goes in v2:
time: 385 us
  waiting for transfers between devices  357 us (93%)
  between operations  13.1 us (3%)
  matrix products  11.5 us (3%)
    reduce_scatter x1, waiting for transfers between devices, shards(): lax.psum_scatter(term * factor, 'tok', scatter_dimension=0, tiled=True)  137 us
    all_gather x1, waiting for transfers between devices, shards(): mixed = jnp.sum(lax.all_gather(partial_rows, axis_name='feat'), 0)  121 us
    all_gather x1, waiting for transfers between devices, shards(): lax.all_gather(weight, 'tok', axis=1, tiled=True)  98.3 us
  transfers between devices with their start and end apart: 3, of which 3 were waited for; matrix products, arithmetic and copies ran while one was open for 0% of the time, Pallas kernels for 0%

profile of v2, /device:TPU:6, one launch (start us, length us, event | category | flops | bytes accessed | tf_op | source)
XLA Modules:
  0.0 384.6 jit_solution(3173620687626841803)
XLA Ops:
  6.5 0.0 copy-start
  6.5 0.0 all-gather.4.cloned.1.call-start
  6.5 0.7 all-gather.4.cloned.1.call-update
  7.3 0.0 all-gather.6.cloned.1.call-start
  7.3 98.3 %all-gather.4.cloned.1.call-done = f32[1792,512]{0,1:T(8,128)} async-done(((f32[1792,16]{0,1:T(8,128)}), f32[1792,512]{0,1:T(8,128)}) %all-gather.4.cloned.1.call-update) | async-done | bytes 3670032 | tf_op jit(solution)/shard_map/all_gather | solution.py:12
  105.6 0.0 copy-done
  105.6 6.6 %fusion = f32[160,512]{1,0:T(8,128)} fusion(f32[160,1792]{1,0:T(8,128)S(1)} %copy-done, f32[1792,512]{0,1:T(8,128)} %all-gather.4.cloned.1.call-done), kind=kOutput, calls=%fused_computation.1 | convolution fusion | flops 1761607680 | bytes 5144576 | tf_op jit(solution)/shard_map/dot_general | solution.py:10
  112.2 0.0 all-gather.6.cloned.1.call-update
  112.2 0.0 reduce-scatter.2.cloned.1.call-start
  112.3 120.7 %all-gather.6.cloned.1.call-done = f32[2560,512]{1,0:T(8,128)} async-done(((f32[160,512]{1,0:T(8,128)}), f32[2560,512]{1,0:T(8,128)}) %all-gather.6.cloned.1.call-update) | async-done | bytes 5242896 | tf_op jit(solution)/shard_map/all_gather | solution.py:16
  233.0 3.1 reduce_sum.9
  236.1 4.9 %convolution_multiply_fusion = f32[512,1792]{1,0:T(8,128)} fusion(f32[160,512]{1,0:T(8,128)S(1)} %reduce_sum.9, f32[160,1792]{1,0:T(8,128)S(1)} %copy-done), kind=kOutput, calls=%fused_computation | convolution fusion | flops 1762525184 | bytes 5144576 | tf_op jit(solution)/shard_map/dot_general | solution.py:18
  241.0 0.0 reduce-scatter.2.cloned.1.call-update
  241.0 137.1 %reduce-scatter.2.cloned.1.call-done = f32[16,1792]{1,0:T(8,128)} async-done(((f32[512,1792]{1,0:T(8,128)}), f32[16,1792]{1,0:T(8,128)}) %reduce-scatter.2.cloned.1.call-update) | async-done | bytes 114704 | tf_op jit(solution)/shard_map/reduce_scatter | solution.py:25
Async XLA Ops:
  6.5 99.1 %copy-start = (f32[160,1792]{1,0:T(8,128)S(1)}, f32[160,1792]{1,0:T(8,128)}, u32[]{:S(2)}) copy-start(f32[160,1792]{1,0:T(8,128)} %param.2) | copy-start | bytes 3440644
  6.5 99.0 %all-gather.4.cloned.1.call-start = ((), (), s32[]{:S(2)}) async-start(), calls=%async_computation.1 | async-start | bytes 3784704 | tf_op jit(solution)/shard_map/all_gather | solution.py:12
  7.3 225.7 %all-gather.6.cloned.1.call-start = ((), (), s32[]{:S(2)}) async-start(), calls=%async_computation.3 | async-start | bytes 5570560 | tf_op jit(solution)/shard_map/all_gather | solution.py:16
  112.2 265.8 %reduce-scatter.2.cloned.1.call-start = ((), (), s32[]{:S(2)}) async-start(), calls=%async_computation.2 | async-start | bytes 3784704 | tf_op jit(solution)/shard_map/reduce_scatter | solution.py:25
Sparse Core Ops, SparseCore 0:
  10.5 95.0 all-gather.3
  112.3 120.6 all-gather.5
  241.1 136.8 reduce-scatter.1
